TPU v7x, 32 devices: a whole 2x2x4 slice. The times are simulated.
32 devices in a mesh: grp: 4 (over z), gz: 8 (over y, x, core).
Axes of the slice: x: 2, y: 2, z: 4, core: 2. Of those that a mesh axis runs over, the one named last changes fastest.
Arguments:
- load: float32 [3, 256, 64, 128], P(None, ('grp', 'gz')), may hold values from -128 to 128
- phases: int32 [256, 64, 128], P(('grp', 'gz')), may hold values from 0 to 3
- clamp: int32 [64, 128], replicated, may hold values 0 or 1
- phase_moduli: float32 [4], replicated, may hold values from 0.05 to 1
Outputs:
- displacement: float32 [3, 256, 64, 128], P(None, ('grp', 'gz'))
- residual: float32 [3, 256, 64, 128], P(None, ('grp', 'gz'))
All inputs are finite; a program needn't handle non-finite values.
Results may differ from a plain program's by a relative error of at most 0.0003.
Values sent between devices are 32-bit elements; how exact they have to be, the bound alone decides.
A program may use at most 128 MiB of HBM per device.

v0:
```python
import math
import jax
import jax.numpy as jnp
import numpy as np
from jax import lax
from jax.sharding import PartitionSpec as P

PHASES = 4
COARSEN = 8
CHEB = 4
ITERS = 2
CORNER_OFFSETS = [
    (along_z, along_y, along_x) for along_z in (0, 1) for along_y in (0, 1) for along_x in (0, 1)
]


def passed_along(value, axis, by):
    size = lax.axis_size(axis)
    pairs = [(i, i + by) for i in range(size) if 0 <= i + by < size]
    return lax.ppermute(value, axis, pairs)


def spread(block, axis, holder):
    block = jnp.where(lax.axis_index(axis) == holder, block, jnp.zeros_like(block))
    return lax.psum(block, axis)


def element_matrix():
    poisson = 0.3
    lame_first = poisson / ((1.0 + poisson) * (1.0 - 2.0 * poisson))
    shear = 1.0 / (2.0 * (1.0 + poisson))
    elastic = np.zeros((6, 6))
    elastic[:3, :3] = lame_first
    for axis_one in range(3):
        elastic[axis_one, axis_one] = lame_first + 2.0 * shear
        elastic[axis_one + 3, axis_one + 3] = shear
    points = [0.5 - 0.5 / math.sqrt(3.0), 0.5 + 0.5 / math.sqrt(3.0)]
    pairs = [(0, 1), (1, 2), (0, 2)]
    matrix = np.zeros((24, 24))
    for first_point in points:
        for second_point in points:
            for third_point in points:
                spot = (first_point, second_point, third_point)
                strain = np.zeros((6, 24))
                for corner, offset in enumerate(CORNER_OFFSETS):
                    values = [
                        spot[axis_one] if offset[axis_one] else 1.0 - spot[axis_one]
                        for axis_one in range(3)
                    ]
                    slopes = [1.0 if offset[axis_one] else -1.0 for axis_one in range(3)]
                    slants = []
                    for axis_one in range(3):
                        others = [values[axis_two] for axis_two in range(3) if axis_two != axis_one]
                        slants.append(slopes[axis_one] * others[0] * others[1])
                        strain[axis_one, 3 * corner + axis_one] = slants[axis_one]
                    for position, pair in enumerate(pairs):
                        strain[3 + position, 3 * corner + pair[0]] = slants[pair[1]]
                        strain[3 + position, 3 * corner + pair[1]] = slants[pair[0]]
                matrix = matrix + 0.125 * (strain.T @ elastic @ strain)
    return matrix


def spectral_bound(numbers):
    diagonal_part = np.array([numbers[index, index] for index in range(numbers.shape[0])])
    return float(np.max(np.sum(np.abs(numbers), axis=1) / diagonal_part))


def element_forces(extended, moduli, matrix):
    layers = moduli.shape[0]
    width = min(4, layers)
    blocks = (layers + width - 1) // width
    plane = tuple(extended.shape[2:])

    def add_block(total, index):
        start = index * width
        nodes = lax.dynamic_slice_in_dim(extended, start, width + 1, 1)
        weights = lax.dynamic_slice_in_dim(moduli, start, width, 0)
        gathered = jnp.stack(
            [
                jnp.roll(nodes[:, along_z : along_z + width], (-along_y, -along_x), (2, 3))
                for along_z, along_y, along_x in CORNER_OFFSETS
            ],
            0,
        )
        gathered = gathered.reshape((24, width) + plane)
        forces = (
            jnp.einsum("ij,jzyx->izyx", matrix, gathered, precision=lax.Precision.HIGHEST) * weights
        )
        forces = forces.reshape((8, 3, width) + plane)
        update = jnp.zeros((3, width + 1) + plane, jnp.float32)
        for corner, offset in enumerate(CORNER_OFFSETS):
            update = update.at[:, offset[0] : offset[0] + width].add(
                jnp.roll(forces[corner], (offset[1], offset[2]), (2, 3))
            )
        current = lax.dynamic_slice_in_dim(total, start, width + 1, 1)
        return (lax.dynamic_update_slice_in_dim(total, current + update, start, 1), None)

    initial = jnp.zeros(extended.shape, jnp.float32)
    total, unused = lax.scan(add_block, initial, jnp.arange(blocks, dtype=jnp.int32))
    return total[:, : layers + 1]


def node_diagonal(lower, moduli, matrix):
    layers = moduli.shape[0]
    extended = jnp.concatenate([lower, moduli], 0)
    entries = jnp.diagonal(matrix).reshape(8, 3)
    total = jnp.zeros((3,) + tuple(moduli.shape), jnp.float32)
    for corner, offset in enumerate(CORNER_OFFSETS):
        shifted = jnp.roll(
            extended[1 - offset[0] : 1 - offset[0] + layers], (offset[1], offset[2]), (1, 2)
        )
        total = total + entries[corner][:, None, None, None] * shifted[None]
    return total


def chebyshev(rhs, coarse_apply, coarse_inverse, bound, sweeps):
    bottom = bound / 20.0
    center = 0.5 * (bound + bottom)
    radius = 0.5 * (bound - bottom)
    sigma = center / radius
    rho = 1.0 / sigma
    update = coarse_inverse * rhs / center
    correction = update
    remainder = rhs
    for sweep in range(sweeps - 1):
        remainder = remainder - coarse_apply(update)
        rho_next = 1.0 / (2.0 * sigma - rho)
        update = rho_next * rho * update + 2.0 * rho_next / radius * coarse_inverse * remainder
        correction = correction + update
        rho = rho_next
    return correction


def restrict(field, factor):
    comps, layers, height, breadth = field.shape
    return field.reshape(
        comps, layers // factor, factor, height // factor, factor, breadth // factor, factor
    ).sum((2, 4, 6))


def prolong(coarse, factor):
    comps, layers, height, breadth = coarse.shape
    expanded = jnp.broadcast_to(
        coarse[:, :, None, :, None, :, None],
        (comps, layers, factor, height, factor, breadth, factor),
    )
    return expanded.reshape(comps, layers * factor, height * factor, breadth * factor)


def paired_sums(residual, preconditioned, image):
    return lax.psum(
        (jnp.sum(residual * preconditioned), jnp.sum(preconditioned * image)), ("grp", "gz")
    )


def body(load, phases, clamp, phase_moduli):
    numbers = element_matrix()
    matrix = jnp.asarray(numbers, jnp.float32)
    bound = spectral_bound(numbers)
    omega = 1.2 / bound
    layers, height, breadth = phases.shape
    factor = COARSEN
    tile = lax.axis_index(("grp", "gz"))
    tiles = lax.axis_size(("grp", "gz"))
    member = lax.axis_index("gz")
    members = lax.axis_size("gz")
    depth = tile * layers + jnp.arange(layers, dtype=jnp.int32)[:, None, None]
    rows_at = jnp.arange(height, dtype=jnp.int32)[None, :, None]
    columns_at = jnp.arange(breadth, dtype=jnp.int32)[None, None, :]
    picked = jnp.zeros((layers, height, breadth), jnp.float32)
    for phase in range(PHASES):
        picked = picked + jnp.where(phases == phase, phase_moduli[phase], jnp.float32(0.0))
    outside = (depth == tiles * layers - 1) | (rows_at == height - 1) | (columns_at == breadth - 1)
    moduli = jnp.where(outside, jnp.float32(0.0), picked)
    free = jnp.where((depth == 0) & (clamp[None] == 1), 0.0, 1.0).astype(jnp.float32)
    lower = passed_along(moduli[-1:], ("grp", "gz"), 1)
    inverse = 1.0 / (free * node_diagonal(lower, moduli, matrix) + 1.0 - free)

    def stiffness(field):
        above = passed_along(field[:, :1], ("grp", "gz"), -1)
        total = element_forces(jnp.concatenate([field, above], 1), moduli, matrix)
        below = passed_along(total[:, -1:], ("grp", "gz"), 1)
        return total[:, :-1].at[:, :1].add(below)

    def operator(field):
        return free * stiffness(free * field) + (1.0 - free) * field

    coarse_layers = layers // factor
    coarse_height = height // factor
    coarse_breadth = breadth // factor
    group_layers = members * coarse_layers
    block_mean = moduli.reshape(
        coarse_layers, factor, coarse_height, factor, coarse_breadth, factor
    ).mean((1, 3, 5))
    coarse_depth = (
        member * coarse_layers + jnp.arange(coarse_layers, dtype=jnp.int32)[:, None, None]
    )
    coarse_rows = jnp.arange(coarse_height, dtype=jnp.int32)[None, :, None]
    coarse_columns = jnp.arange(coarse_breadth, dtype=jnp.int32)[None, None, :]
    coarse_edge = (
        (coarse_depth == group_layers - 1)
        | (coarse_rows == coarse_height - 1)
        | (coarse_columns == coarse_breadth - 1)
    )
    coarse_local = jnp.where(coarse_edge, jnp.float32(0.0), block_mean)
    group_moduli = lax.all_gather(coarse_local, "gz", axis=0, tiled=True)
    coarse_matrix = factor * matrix
    coarse_bottom = jnp.zeros((1, coarse_height, coarse_breadth), jnp.float32)
    coarse_top = jnp.zeros((3, 1, coarse_height, coarse_breadth), jnp.float32)
    coarse_inverse = 1.0 / node_diagonal(coarse_bottom, group_moduli, coarse_matrix)

    def coarse_apply(field):
        return element_forces(jnp.concatenate([field, coarse_top], 1), group_moduli, coarse_matrix)[
            :, :-1
        ]

    def solve_group(summed):
        return chebyshev(summed, coarse_apply, coarse_inverse, bound, CHEB)

    def blank_group(summed):
        return jnp.zeros_like(summed)

    def precondition(current):
        first = omega * current * inverse
        defect = current - operator(first)
        restricted = restrict(defect, factor)
        summed = lax.all_gather(restricted, "gz", axis=1, tiled=True)
        solved = lax.cond(member == 0, solve_group, blank_group, summed)
        solved = spread(solved, "gz", 0)
        own = lax.dynamic_slice_in_dim(solved, member * coarse_layers, coarse_layers, 1)
        second = first + free * prolong(own, factor)
        return second + omega * (current - operator(second)) * inverse

    rhs = free * load
    displacement = jnp.zeros_like(rhs)
    residual = rhs
    preconditioned = precondition(residual)
    image = operator(preconditioned)
    gamma, curve = paired_sums(residual, preconditioned, image)
    alpha = gamma / curve
    direction = preconditioned
    along = image
    for step in range(ITERS):
        displacement = displacement + alpha * direction
        residual = residual - alpha * along
        if step + 1 < ITERS:
            preconditioned = precondition(residual)
            image = operator(preconditioned)
            following, curve = paired_sums(residual, preconditioned, image)
            beta = following / gamma
            alpha = following / (curve - beta * following / alpha)
            direction = preconditioned + beta * direction
            along = image + beta * along
            gamma = following
    return (displacement, residual)


def solution(mesh):
    placed = (P(None, ("grp", "gz"), None, None), P(("grp", "gz"), None, None), P(), P())
    return jax.shard_map(
        body,
        mesh=mesh,
        in_specs=placed,
        out_specs=(P(None, ("grp", "gz"), None, None), P(None, ("grp", "gz"), None, None)),
        check_vma=False,
    )
```

profile of v0, /device:TPU:0, one launch (start us, length us, event | category | flops | bytes accessed | tf_op | source)
XLA Modules:
  0.0 781.7 jit_solution(1037202731570324370)
XLA Ops:
  8.7 12.1 %all_gather.9 = f32[8,8,16]{2,1,0:T(8,128)} all-gather(f32[1,8,16]{2,1,0:T(8,128)S(1)} %bitcast_select_fusion), channel_id=1, replica_groups=mesh['grp'=4,'gz'=8] {'gz'}, dimensions={0}, use_global_device_ids=true | all-gather | bytes 4608 | tf_op jit(solution)/shard_map/all_gather | solution.py:206
  36.3 44.2 %while.252 = (s32[]{:T(128)}, f32[3,9,64,128]{3,2,1,0:T(8,128)}, s32[2]{0:T(128)S(1)}, f32[3,9,64,128]{3,2,1,0:T(8,128)S(1)}, f32[8,64,128]{2,1,0:T(8,128)S(1)},...) while((s32[]{:T(128)}, f32[3,9,64,128]{3,2,1,0:T(8,128)}, ...), condition=%wide.region_3.4_spmd.clone, body=%wide.region_2.3_spmd.sunk.clone.sunk | while | flops 230057488 | bytes 52208232 | solution.py:99
  45.3 6.5 multiply_bitcast_fusion.12
  67.4 6.5 multiply_bitcast_fusion.12
  92.5 9.1 %all-gather = f32[3,64,16]{2,1,0:T(8,128)S(1)} all-gather(f32[3,8,16]{2,1,0:T(8,128)S(1)} %reduce_sum.93), channel_id=2, replica_groups=mesh['grp'=4,'gz'=8] {'gz'}, dimensions={1}, use_global_device_ids=true | all-gather | bytes 13824 | tf_op jit(solution)/shard_map/all_gather | solution.py:227
  101.7 105.1 %conditional.2 = (f32[3,8,8,16]{3,2,0,1:T(8,128)}) conditional(s32[]{:T(128)} %convert_element_type.4, () %tuple.572, (f32[3,8,8,16]{0,3,2,1:T(8,128)S(1)}, f32[3,8,8,16]{3,2,1,0:T(8,128)S(1)}, f32[24,24]{1,0:T(8,128)S(1)}, f32[8,8,16]{2,1,0:T(8,128)}) %tuple.1309), branch_computations={%region_6.7_spmd, %region_7.14_spmd} | conditional | flops 10876638 | bytes 24754408 | solution.py:228
  104.3 30.9 %while.246 = (s32[]{:T(128)}, f32[3,9,8,16]{0,3,2,1:T(8,128)}, s32[2]{0:T(128)S(1)}, f32[3,9,8,16]{3,2,1,0:T(8,128)S(1)}, f32[24,24]{1,0:T(8,128)S(1)}, /*index=...) while((s32[]{:T(128)}, f32[3,9,8,16]{0,3,2,1:T(8,128)}, ...), condition=%wide.region_9.9_spmd, body=%wide.region_8.8_spmd.sunk | while | flops 3594826 | bytes 8055736 | solution.py:99
  138.7 30.9 %while.247 = (s32[]{:T(128)}, f32[3,9,8,16]{0,3,2,1:T(8,128)}, s32[2]{0:T(128)S(1)}, f32[3,9,8,16]{3,2,1,0:T(8,128)S(1)}, f32[24,24]{1,0:T(8,128)S(1)}, /*index=...) while((s32[]{:T(128)}, f32[3,9,8,16]{0,3,2,1:T(8,128)}, ...), condition=%wide.region_11.11_spmd, body=%wide.region_10.10_spmd.sunk | while | flops 3594826 | bytes 8055736 | solution.py:99
  172.7 31.0 %while.248 = (s32[]{:T(128)}, f32[3,9,8,16]{0,3,2,1:T(8,128)}, s32[2]{0:T(128)S(1)}, f32[3,9,8,16]{3,2,1,0:T(8,128)S(1)}, f32[24,24]{1,0:T(8,128)S(1)}, /*index=...) while((s32[]{:T(128)}, f32[3,9,8,16]{0,3,2,1:T(8,128)}, ...), condition=%wide.region_13.13_spmd, body=%wide.region_12.12_spmd.sunk | while | flops 3594826 | bytes 8055736 | solution.py:99
  207.8 23.2 %psum.42 = f32[3,8,8,16]{3,2,0,1:T(8,128)S(1)} all-reduce(f32[3,8,8,16]{3,2,0,1:T(8,128)S(1)} %broadcast_select_fusion.1), channel_id=1, replica_groups=mesh['grp'=4,'gz'=8] {'gz'}, use_global_device_ids=true, to_apply=%region_14.15 | all-reduce | flops 3072 | bytes 24576 | tf_op jit(solution)/shard_map/psum | solution.py:25
  238.9 44.2 %while.253 = (s32[]{:T(128)}, f32[3,9,64,128]{3,2,1,0:T(8,128)}, s32[2]{0:T(128)S(1)}, f32[3,9,64,128]{3,2,1,0:T(8,128)S(1)}, f32[8,64,128]{2,1,0:T(8,128)S(1)},...) while((s32[]{:T(128)}, f32[3,9,64,128]{3,2,1,0:T(8,128)}, ...), condition=%wide.region_16.17_spmd.clone, body=%wide.region_15.16_spmd.sunk.clone.sunk | while | flops 230057488 | bytes 52208232 | solution.py:99
  247.9 6.5 multiply_bitcast_fusion.13
  270.1 6.5 multiply_bitcast_fusion.13
  295.7 44.2 %while.254 = (s32[]{:T(128)}, f32[3,9,64,128]{3,2,1,0:T(8,128)}, s32[2]{0:T(128)S(1)}, f32[3,9,64,128]{3,2,1,0:T(8,128)S(1)}, f32[8,64,128]{2,1,0:T(8,128)S(1)},...) while((s32[]{:T(128)}, f32[3,9,64,128]{3,2,1,0:T(8,128)}, ...), condition=%wide.region_20.21_spmd.clone, body=%wide.region_19.20_spmd.sunk.clone.sunk | while | flops 230057488 | bytes 52208232 | solution.py:99
  304.8 6.5 multiply_bitcast_fusion.14
  326.9 6.5 multiply_bitcast_fusion.14
  351.1 46.4 %all-reduce.20 = (f32[]{:T(128)}, f32[]{:T(128)}) all-reduce(f32[]{:T(128)} %get-tuple-element.2475, f32[]{:T(128)} %get-tuple-element.2474), channel_id=1, replica_groups=mesh['grp'=4,'gz'=8] {'grp','gz'}, use_global_device_ids=true, to_apply=%region_18.19 | all-reduce | flops 2 | bytes 16 | tf_op jit(solution)/shard_map/psum | solution.py:151
  407.5 44.5 %while.255 = (s32[]{:T(128)}, f32[3,9,64,128]{3,2,1,0:T(8,128)}, s32[2]{0:T(128)S(1)}, f32[3,9,64,128]{3,2,1,0:T(8,128)S(1)}, f32[8,64,128]{2,1,0:T(8,128)S(1)},...) while((s32[]{:T(128)}, f32[3,9,64,128]{3,2,1,0:T(8,128)}, ...), condition=%wide.region_24.25_spmd.clone, body=%wide.region_23.24_spmd.sunk.clone.sunk | while | flops 230057488 | bytes 52208232 | solution.py:99
  416.6 6.5 multiply_bitcast_fusion.15
  465.8 11.1 %all-gather.1 = f32[3,64,16]{2,1,0:T(8,128)S(1)} all-gather(f32[3,8,16]{2,1,0:T(8,128)S(1)} %reduce_sum.99), channel_id=3, replica_groups=mesh['grp'=4,'gz'=8] {'gz'}, dimensions={1}, use_global_device_ids=true | all-gather | bytes 13824 | tf_op jit(solution)/shard_map/all_gather | solution.py:227
  477.0 105.4 %conditional.3 = (f32[3,8,8,16]{3,2,0,1:T(8,128)}) conditional(s32[]{:T(128)} %convert_element_type.4, () %tuple.577, (f32[3,8,8,16]{0,3,2,1:T(8,128)S(1)}, f32[3,8,8,16]{3,2,1,0:T(8,128)S(1)}, f32[24,24]{1,0:T(8,128)S(1)}, f32[8,8,16]{2,1,0:T(8,128)}) %tuple.1308), branch_computations={%region_27.28_spmd, %region_28.35_spmd} | conditional | flops 10876638 | bytes 24754408 | solution.py:228
  479.6 30.8 %while.249 = (s32[]{:T(128)}, f32[3,9,8,16]{0,3,2,1:T(8,128)}, s32[2]{0:T(128)S(1)}, f32[3,9,8,16]{3,2,1,0:T(8,128)S(1)}, f32[24,24]{1,0:T(8,128)S(1)}, /*index=...) while((s32[]{:T(128)}, f32[3,9,8,16]{0,3,2,1:T(8,128)}, ...), condition=%wide.region_30.30_spmd, body=%wide.region_29.29_spmd.sunk | while | flops 3594826 | bytes 8055736 | solution.py:99
  513.9 31.2 %while.250 = (s32[]{:T(128)}, f32[3,9,8,16]{0,3,2,1:T(8,128)}, s32[2]{0:T(128)S(1)}, f32[3,9,8,16]{3,2,1,0:T(8,128)S(1)}, f32[24,24]{1,0:T(8,128)S(1)}, /*index=...) while((s32[]{:T(128)}, f32[3,9,8,16]{0,3,2,1:T(8,128)}, ...), condition=%wide.region_32.32_spmd, body=%wide.region_31.31_spmd.sunk | while | flops 3594826 | bytes 8055736 | solution.py:99
  548.1 31.2 %while.251 = (s32[]{:T(128)}, f32[3,9,8,16]{0,3,2,1:T(8,128)}, s32[2]{0:T(128)S(1)}, f32[3,9,8,16]{3,2,1,0:T(8,128)S(1)}, f32[24,24]{1,0:T(8,128)S(1)}, /*index=...) while((s32[]{:T(128)}, f32[3,9,8,16]{0,3,2,1:T(8,128)}, ...), condition=%wide.region_34.34_spmd, body=%wide.region_33.33_spmd.sunk | while | flops 3594826 | bytes 8055736 | solution.py:99
  583.3 23.2 %psum.45 = f32[3,8,8,16]{3,2,0,1:T(8,128)S(1)} all-reduce(f32[3,8,8,16]{3,2,0,1:T(8,128)S(1)} %broadcast_select_fusion), channel_id=1, replica_groups=mesh['grp'=4,'gz'=8] {'gz'}, use_global_device_ids=true, to_apply=%region_35.36 | all-reduce | flops 3072 | bytes 24576 | tf_op jit(solution)/shard_map/psum | solution.py:25
  614.4 44.4 %while.256 = (s32[]{:T(128)}, f32[3,9,64,128]{3,2,1,0:T(8,128)}, s32[2]{0:T(128)S(1)}, f32[3,9,64,128]{3,2,1,0:T(8,128)S(1)}, f32[8,64,128]{2,1,0:T(8,128)S(1)},...) while((s32[]{:T(128)}, f32[3,9,64,128]{3,2,1,0:T(8,128)}, ...), condition=%wide.region_37.38_spmd.clone, body=%wide.region_36.37_spmd.sunk.clone.sunk | while | flops 230057488 | bytes 52208232 | solution.py:99
  623.6 6.5 multiply_bitcast_fusion.16
  645.8 6.5 multiply_bitcast_fusion.16
  671.1 44.4 %while.257 = (s32[]{:T(128)}, f32[3,9,64,128]{3,2,1,0:T(8,128)}, s32[2]{0:T(128)S(1)}, f32[3,9,64,128]{3,2,1,0:T(8,128)S(1)}, f32[8,64,128]{2,1,0:T(8,128)S(1)},...) while((s32[]{:T(128)}, f32[3,9,64,128]{3,2,1,0:T(8,128)}, ...), condition=%wide.region_41.42_spmd.clone, body=%wide.region_40.41_spmd.sunk.clone.sunk | while | flops 230057488 | bytes 52208232 | solution.py:99
  680.2 6.5 multiply_bitcast_fusion.17
  702.5 6.5 multiply_bitcast_fusion.17
  727.4 46.4 %all-reduce.19 = (f32[]{:T(128)}, f32[]{:T(128)}) all-reduce(f32[]{:T(128)} %get-tuple-element.2477, f32[]{:T(128)} %get-tuple-element.2476), channel_id=1, replica_groups=mesh['grp'=4,'gz'=8] {'grp','gz'}, use_global_device_ids=true, to_apply=%region_39.40 | all-reduce | flops 2 | bytes 16 | tf_op jit(solution)/shard_map/psum | solution.py:151
  (1331 shorter events, 509.9 us)
Async XLA Ops:
  0.6 26.0 %copy-start.16 = (f32[24,24]{1,0:T(8,128)S(1)}, f32[24,24]{1,0:T(8,128)}, u32[]{:S(2)}) copy-start(f32[24,24]{1,0:T(8,128)} %constant.3032.clone) | copy-start | bytes 6916
  0.6 27.4 %copy-start = (f32[24,24]{1,0:T(8,128)S(1)}, f32[24,24]{1,0:T(8,128)}, u32[]{:S(2)}) copy-start(f32[24,24]{1,0:T(8,128)} %constant.3073) | copy-start | bytes 6916
  5.8 24.0 %collective-permute-start = (f32[1,64,128]{2,1,0:T(8,128)S(1)}, f32[1,64,128]{2,1,0:T(8,128)S(1)}, u32[]{:S(2)}, u32[]{:S(2)}) collective-permute-start(f32[1,64,128]{2,1,0:T(8,128)S(1)} %slice.6742), channel_id=1, source_target_pairs={{0,1},{1,2},{2,3},{3,4},{4,5},{5,6},{6,7},{7,8},{8,9},{9,10},{10,1... | collective-permute-start | bytes 98312 | tf_op jit(solution)/shard_map/ppermute | solution.py:20
  29.6 61.6 %copy-start.17 = (f32[8,64,128]{2,1,0:T(8,128)}, f32[8,64,128]{2,1,0:T(8,128)S(1)}, u32[]{:S(2)}) copy-start(f32[8,64,128]{2,1,0:T(8,128)S(1)} %get-tuple-element.2978) | copy-start | bytes 786436
  32.0 3.2 collective-permute-start.1
  36.3 50.6 %copy-start.70 = (f32[3]{0:T(128)S(1)}, f32[3]{0:T(128)}, u32[]{:S(2)}) copy-start(f32[3]{0:T(128)} %get-tuple-element.2986) | copy-start | bytes 40
  36.3 50.6 %copy-start.71 = (f32[3]{0:T(128)S(1)}, f32[3]{0:T(128)}, u32[]{:S(2)}) copy-start(f32[3]{0:T(128)} %get-tuple-element.2987) | copy-start | bytes 40
  80.5 10.7 %copy-start.5 = (f32[3,8,64,128]{3,2,1,0:T(8,128)S(1)}, f32[3,8,64,128]{3,2,1,0:T(8,128)}, u32[]{:S(2)}) copy-start(f32[3,8,64,128]{3,2,1,0:T(8,128)} %param.237) | copy-start | bytes 2359300
  81.5 8.8 %collective-permute-start.2 = (f32[3,1,64,128]{3,2,1,0:T(8,128)S(1)}, f32[3,1,64,128]{3,2,1,0:T(8,128)S(1)}, u32[]{:S(2)}, u32[]{:S(2)}) collective-permute-start(f32[3,1,64,128]{3,2,1,0:T(8,128)S(1)} %slice.5989), channel_id=1, source_target_pairs={{0,1},{1,2},{2,3},{3,4},{4,5},{5,6},{6,7},{7,8},{8,9},{9,10},{10,1... | collective-permute-start | bytes 294920 | tf_op jit(solution)/shard_map/ppermute | solution.py:20
  88.8 12.9 %copy-start.2 = (f32[3,8,8,16]{0,3,2,1:T(8,128)}, f32[3,8,8,16]{0,3,2,1:T(8,128)S(1)}, u32[]{:S(2)}) copy-start(f32[3,8,8,16]{0,3,2,1:T(8,128)S(1)} %add_divide_fusion) | copy-start | bytes 36868
  206.8 27.6 %copy-start.6 = (f32[3,8,64,128]{3,2,1,0:T(8,128)S(1)}, f32[3,8,64,128]{3,2,1,0:T(8,128)}, u32[]{:S(2)}) copy-start(f32[3,8,64,128]{3,2,1,0:T(8,128)} %param.237) | copy-start | bytes 2359300
  234.6 3.2 collective-permute-start.3
  238.9 50.1 %copy-start.18 = (f32[8,64,128]{2,1,0:T(8,128)S(1)}, f32[8,64,128]{2,1,0:T(8,128)}, u32[]{:S(2)}) copy-start(f32[8,64,128]{2,1,0:T(8,128)} %copy-done.17) | copy-start | bytes 786436
  284.0 4.1 collective-permute-start.4
  291.4 3.2 collective-permute-start.5
  340.0 58.8 %copy-start.7 = (f32[3,8,64,128]{3,2,1,0:T(8,128)S(1)}, f32[3,8,64,128]{3,2,1,0:T(8,128)}, u32[]{:S(2)}) copy-start(f32[3,8,64,128]{3,2,1,0:T(8,128)} %param.237) | copy-start | bytes 2359300
  341.0 6.7 collective-permute-start.6
  348.6 52.6 %copy-start.34 = (f32[3,8,64,128]{3,2,1,0:T(8,128)}, f32[3,8,64,128]{3,2,1,0:T(8,128)S(1)}, u32[]{:S(2)}) copy-start(f32[3,8,64,128]{3,2,1,0:T(8,128)S(1)} %add_dynamic-update-slice_fusion.21) | copy-start | bytes 2359300
  402.1 3.2 collective-permute-start.7
  451.9 12.3 %copy-start.39 = (f32[24,24,1,1]{1,0,3,2:T(8,128)}, f32[24,24,1,1]{1,0,3,2:T(8,128)S(1)}, u32[]{:S(2)}) copy-start(f32[24,24,1,1]{1,0,3,2:T(8,128)S(1)} %get-tuple-element.4566) | copy-start | bytes 6916
  452.9 6.9 collective-permute-start.8
  460.7 16.2 %copy-start.1 = (f32[24,24]{1,0:T(8,128)S(1)}, f32[24,24]{1,0:T(8,128)}, u32[]{:S(2)}) copy-start(f32[24,24]{1,0:T(8,128)} %constant.3073) | copy-start | bytes 6916
  460.7 16.2 %copy-start.3 = (f32[3,8,8,16]{0,3,2,1:T(8,128)S(1)}, f32[3,8,8,16]{0,3,2,1:T(8,128)}, u32[]{:S(2)}) copy-start(f32[3,8,8,16]{0,3,2,1:T(8,128)} %copy-done.2) | copy-start | bytes 36868
  582.3 27.6 %copy-start.8 = (f32[3,8,64,128]{3,2,1,0:T(8,128)S(1)}, f32[3,8,64,128]{3,2,1,0:T(8,128)}, u32[]{:S(2)}) copy-start(f32[3,8,64,128]{3,2,1,0:T(8,128)} %get-tuple-element.2665) | copy-start | bytes 2359300
  610.1 3.2 collective-permute-start.9
  614.4 49.9 %copy-start.19 = (f32[8,64,128]{2,1,0:T(8,128)S(1)}, f32[8,64,128]{2,1,0:T(8,128)}, u32[]{:S(2)}) copy-start(f32[8,64,128]{2,1,0:T(8,128)} %copy-done.17) | copy-start | bytes 786436
  659.8 3.7 collective-permute-start.10
  666.8 3.2 collective-permute-start.11
  671.1 54.2 %copy-start.9 = (f32[3,8,64,128]{3,2,1,0:T(8,128)S(1)}, f32[3,8,64,128]{3,2,1,0:T(8,128)}, u32[]{:S(2)}) copy-start(f32[3,8,64,128]{3,2,1,0:T(8,128)} %get-tuple-element.2665) | copy-start | bytes 2359300
  715.6 62.8 %copy-start.35 = (f32[3,8,64,128]{3,2,1,0:T(8,128)S(1)}, f32[3,8,64,128]{3,2,1,0:T(8,128)}, u32[]{:S(2)}) copy-start(f32[3,8,64,128]{3,2,1,0:T(8,128)} %copy-done.34) | copy-start | bytes 2359300
  715.6 62.8 %copy-start.36 = (f32[3,8,64,128]{3,2,1,0:T(8,128)S(1)}, f32[3,8,64,128]{3,2,1,0:T(8,128)}, u32[]{:S(2)}) copy-start(f32[3,8,64,128]{3,2,1,0:T(8,128)} %get-tuple-element.2667) | copy-start | bytes 2359300
  716.6 6.9 collective-permute-start.12
  (103 other events, 147.6 us)
where the time goes:
time: 792 us; the launch traced here: 782 us
  other arithmetic  226 us (29%)
  local copies, waits for them, and re-layouts  217 us (27%)
  blocking collectives  171 us (22%)
  matrix products  89.6 us (11%)
  starting transfers between devices  38.5 us (5%)
  loops' own time  20.7 us (3%)
  waiting for transfers between devices  10.6 us (1%)
    psum x2, blocking collectives, paired_sums(): lax.psum((jnp.sum(residual * preconditioned), jnp.sum(preconditioned * im...  92.8 us
    dot_general x24, matrix products, add_block(): jnp.einsum('ij,jzyx->izyx', matrix, gathered, precision=lax.Precision.HIG...  89.6 us
    slice x144, local copies, waits for them, and re-layouts, add_block(): jnp.roll(forces[corner], (offset[1], offset[2]), (2, 3))  72.7 us
    while x120, other arithmetic  55.6 us
    scatter-add x144, other arithmetic, add_block(): update.at[:, offset[0]:offset[0] + width]  55.2 us
    psum x2, blocking collectives, spread(): return lax.psum(block, axis)  46.3 us
    ppermute x13, starting transfers between devices, passed_along(): return lax.ppermute(value, axis, pairs)  38.5 us
    while x216, local copies, waits for them, and re-layouts  37.6 us
  transfers between devices with their start and end apart: 13, of which 6 were waited for; matrix products, arithmetic and copies ran while one was open for 2% of the time, Pallas kernels for 0%

commit v1 on v0

--- a/solution.py
+++ b/solution.py
@@ -22,7 +22,7 @@
 
 def spread(block, axis, holder):
     block = jnp.where(lax.axis_index(axis) == holder, block, jnp.zeros_like(block))
-    return lax.psum(block, axis)
+    return jnp.sum(lax.all_gather(block, axis), axis=0)
 
 
 def element_matrix():

time: 792 us -> 768 us (0.970)
  blocking collectives: 171 us -> 142 us
    psum x2 -> x0, blocking collectives: 46.3 us -> none  [spread(): return lax.psum(block, axis)]
    all_gather x0 -> x2, blocking collectives: none -> 19.1 us  [spread(): return jnp.sum(lax.all_gather(block, axis), axis=0)]
where the time goes in v1:
time: 768 us; the launch traced here: 757 us
  other arithmetic  227 us (30%)
  local copies, waits for them, and re-layouts  217 us (28%)
  blocking collectives  142 us (18%)
  matrix products  89.6 us (12%)
  starting transfers between devices  43.5 us (6%)
  loops' own time  20.7 us (3%)
  waiting for transfers between devices  10.7 us (1%)
    psum x2, blocking collectives, paired_sums(): lax.psum((jnp.sum(residual * preconditioned), jnp.sum(preconditioned * im...  90.4 us
    dot_general x24, matrix products, add_block(): jnp.einsum('ij,jzyx->izyx', matrix, gathered, precision=lax.Precision.HIG...  89.6 us
    slice x144, local copies, waits for them, and re-layouts, add_block(): jnp.roll(forces[corner], (offset[1], offset[2]), (2, 3))  72.7 us
    while x120, other arithmetic  55.6 us
    scatter-add x144, other arithmetic, add_block(): update.at[:, offset[0]:offset[0] + width]  55.2 us
    ppermute x13, starting transfers between devices, passed_along(): return lax.ppermute(value, axis, pairs)  43.5 us
    while x216, local copies, waits for them, and re-layouts  37.6 us
    dynamic_update_slice x12, other arithmetic, add_block(): lax.dynamic_update_slice_in_dim(total, current + update, start, 1)  21.2 us
  transfers between devices with their start and end apart: 13, of which 6 were waited for; matrix products, arithmetic and copies ran while one was open for 2% of the time, Pallas kernels for 0%

profile of v1, /device:TPU:0, one launch (start us, length us, event | category | flops | bytes accessed | tf_op | source)
XLA Modules:
  0.0 757.3 jit_solution(10361939107030790206)
XLA Ops:
  8.7 12.1 %all_gather.21 = f32[8,8,16]{2,1,0:T(8,128)} all-gather(f32[1,8,16]{2,1,0:T(8,128)S(1)} %bitcast_select_fusion), channel_id=1, replica_groups=mesh['grp'=4,'gz'=8] {'gz'}, dimensions={0}, use_global_device_ids=true | all-gather | bytes 4608 | tf_op jit(solution)/shard_map/all_gather | solution.py:206
  36.3 44.2 %while.252 = (s32[]{:T(128)}, f32[3,9,64,128]{3,2,1,0:T(8,128)}, s32[2]{0:T(128)S(1)}, f32[3,9,64,128]{3,2,1,0:T(8,128)S(1)}, f32[8,64,128]{2,1,0:T(8,128)S(1)},...) while((s32[]{:T(128)}, f32[3,9,64,128]{3,2,1,0:T(8,128)}, ...), condition=%wide.region_3.4_spmd.clone, body=%wide.region_2.3_spmd.sunk.clone.sunk | while | flops 230057488 | bytes 52208232 | solution.py:99
  45.3 6.5 multiply_bitcast_fusion.12
  67.4 6.5 multiply_bitcast_fusion.12
  92.5 9.1 %all-gather = f32[3,64,16]{2,1,0:T(8,128)S(1)} all-gather(f32[3,8,16]{2,1,0:T(8,128)S(1)} %reduce_sum.111), channel_id=2, replica_groups=mesh['grp'=4,'gz'=8] {'gz'}, dimensions={1}, use_global_device_ids=true | all-gather | bytes 13824 | tf_op jit(solution)/shard_map/all_gather | solution.py:227
  101.7 105.2 %conditional.2 = (f32[3,8,8,16]{3,2,1,0:T(8,128)}) conditional(s32[]{:T(128)} %convert_element_type.4, () %tuple.572, (f32[3,8,8,16]{0,3,2,1:T(8,128)S(1)}, f32[3,8,8,16]{3,2,1,0:T(8,128)S(1)}, f32[24,24]{1,0:T(8,128)S(1)}, f32[8,8,16]{2,1,0:T(8,128)}) %tuple.1309), branch_computations={%region_6.7_spmd, %region_7.14_spmd} | conditional | flops 10876638 | bytes 24754408 | solution.py:228
  104.3 30.9 %while.246 = (s32[]{:T(128)}, f32[3,9,8,16]{0,3,2,1:T(8,128)}, s32[2]{0:T(128)S(1)}, f32[3,9,8,16]{3,2,1,0:T(8,128)S(1)}, f32[24,24]{1,0:T(8,128)S(1)}, /*index=...) while((s32[]{:T(128)}, f32[3,9,8,16]{0,3,2,1:T(8,128)}, ...), condition=%wide.region_9.9_spmd, body=%wide.region_8.8_spmd.sunk | while | flops 3594826 | bytes 8055736 | solution.py:99
  138.7 30.9 %while.247 = (s32[]{:T(128)}, f32[3,9,8,16]{0,3,2,1:T(8,128)}, s32[2]{0:T(128)S(1)}, f32[3,9,8,16]{3,2,1,0:T(8,128)S(1)}, f32[24,24]{1,0:T(8,128)S(1)}, /*index=...) while((s32[]{:T(128)}, f32[3,9,8,16]{0,3,2,1:T(8,128)}, ...), condition=%wide.region_11.11_spmd, body=%wide.region_10.10_spmd.sunk | while | flops 3594826 | bytes 8055736 | solution.py:99
  172.7 31.0 %while.248 = (s32[]{:T(128)}, f32[3,9,8,16]{0,3,2,1:T(8,128)}, s32[2]{0:T(128)S(1)}, f32[3,9,8,16]{3,2,1,0:T(8,128)S(1)}, f32[24,24]{1,0:T(8,128)S(1)}, /*index=...) while((s32[]{:T(128)}, f32[3,9,8,16]{0,3,2,1:T(8,128)}, ...), condition=%wide.region_13.13_spmd, body=%wide.region_12.12_spmd.sunk | while | flops 3594826 | bytes 8055736 | solution.py:99
  207.8 9.5 %all-gather.1 = f32[24,8,8,16]{3,2,1,0:T(8,128)S(1)} all-gather(f32[3,8,8,16]{3,2,1,0:T(8,128)S(1)} %broadcast_select_fusion.1), channel_id=3, replica_groups=mesh['grp'=4,'gz'=8] {'gz'}, dimensions={0}, use_global_device_ids=true | all-gather | bytes 110592 | tf_op jit(solution)/shard_map/all_gather | solution.py:25
  225.3 44.2 %while.253 = (s32[]{:T(128)}, f32[3,9,64,128]{3,2,1,0:T(8,128)}, s32[2]{0:T(128)S(1)}, f32[3,9,64,128]{3,2,1,0:T(8,128)S(1)}, f32[8,64,128]{2,1,0:T(8,128)S(1)},...) while((s32[]{:T(128)}, f32[3,9,64,128]{3,2,1,0:T(8,128)}, ...), condition=%wide.region_16.17_spmd.clone, body=%wide.region_15.16_spmd.sunk.clone.sunk | while | flops 230057488 | bytes 52208232 | solution.py:99
  234.3 6.5 multiply_bitcast_fusion.13
  284.6 44.2 %while.254 = (s32[]{:T(128)}, f32[3,9,64,128]{3,2,1,0:T(8,128)}, s32[2]{0:T(128)S(1)}, f32[3,9,64,128]{3,2,1,0:T(8,128)S(1)}, f32[8,64,128]{2,1,0:T(8,128)S(1)},...) while((s32[]{:T(128)}, f32[3,9,64,128]{3,2,1,0:T(8,128)}, ...), condition=%wide.region_20.21_spmd.clone, body=%wide.region_19.20_spmd.sunk.clone.sunk | while | flops 230057488 | bytes 52208232 | solution.py:99
  293.7 6.5 multiply_bitcast_fusion.14
  315.8 6.5 multiply_bitcast_fusion.14
  340.0 45.2 %all-reduce.20 = (f32[]{:T(128)}, f32[]{:T(128)}) all-reduce(f32[]{:T(128)} %get-tuple-element.2475, f32[]{:T(128)} %get-tuple-element.2474), channel_id=1, replica_groups=mesh['grp'=4,'gz'=8] {'grp','gz'}, use_global_device_ids=true, to_apply=%region_18.19 | all-reduce | flops 2 | bytes 16 | tf_op jit(solution)/shard_map/psum | solution.py:151
  395.2 44.5 %while.255 = (s32[]{:T(128)}, f32[3,9,64,128]{3,2,1,0:T(8,128)}, s32[2]{0:T(128)S(1)}, f32[3,9,64,128]{3,2,1,0:T(8,128)S(1)}, f32[8,64,128]{2,1,0:T(8,128)S(1)},...) while((s32[]{:T(128)}, f32[3,9,64,128]{3,2,1,0:T(8,128)}, ...), condition=%wide.region_24.25_spmd.clone, body=%wide.region_23.24_spmd.sunk.clone.sunk | while | flops 230057488 | bytes 52208232 | solution.py:99
  404.3 6.5 multiply_bitcast_fusion.15
  426.5 6.5 multiply_bitcast_fusion.15
  453.5 11.1 %all-gather.2 = f32[3,64,16]{2,1,0:T(8,128)S(1)} all-gather(f32[3,8,16]{2,1,0:T(8,128)S(1)} %reduce_sum.118), channel_id=4, replica_groups=mesh['grp'=4,'gz'=8] {'gz'}, dimensions={1}, use_global_device_ids=true | all-gather | bytes 13824 | tf_op jit(solution)/shard_map/all_gather | solution.py:227
  464.6 105.4 %conditional.3 = (f32[3,8,8,16]{3,2,1,0:T(8,128)}) conditional(s32[]{:T(128)} %convert_element_type.4, () %tuple.577, (f32[3,8,8,16]{0,3,2,1:T(8,128)S(1)}, f32[3,8,8,16]{3,2,1,0:T(8,128)S(1)}, f32[24,24]{1,0:T(8,128)S(1)}, f32[8,8,16]{2,1,0:T(8,128)}) %tuple.1308), branch_computations={%region_27.28_spmd, %region_28.35_spmd} | conditional | flops 10876638 | bytes 24754408 | solution.py:228
  467.2 30.8 %while.249 = (s32[]{:T(128)}, f32[3,9,8,16]{0,3,2,1:T(8,128)}, s32[2]{0:T(128)S(1)}, f32[3,9,8,16]{3,2,1,0:T(8,128)S(1)}, f32[24,24]{1,0:T(8,128)S(1)}, /*index=...) while((s32[]{:T(128)}, f32[3,9,8,16]{0,3,2,1:T(8,128)}, ...), condition=%wide.region_30.30_spmd, body=%wide.region_29.29_spmd.sunk | while | flops 3594826 | bytes 8055736 | solution.py:99
  501.5 31.2 %while.250 = (s32[]{:T(128)}, f32[3,9,8,16]{0,3,2,1:T(8,128)}, s32[2]{0:T(128)S(1)}, f32[3,9,8,16]{3,2,1,0:T(8,128)S(1)}, f32[24,24]{1,0:T(8,128)S(1)}, /*index=...) while((s32[]{:T(128)}, f32[3,9,8,16]{0,3,2,1:T(8,128)}, ...), condition=%wide.region_32.32_spmd, body=%wide.region_31.31_spmd.sunk | while | flops 3594826 | bytes 8055736 | solution.py:99
  535.8 31.2 %while.251 = (s32[]{:T(128)}, f32[3,9,8,16]{0,3,2,1:T(8,128)}, s32[2]{0:T(128)S(1)}, f32[3,9,8,16]{3,2,1,0:T(8,128)S(1)}, f32[24,24]{1,0:T(8,128)S(1)}, /*index=...) while((s32[]{:T(128)}, f32[3,9,8,16]{0,3,2,1:T(8,128)}, ...), condition=%wide.region_34.34_spmd, body=%wide.region_33.33_spmd.sunk | while | flops 3594826 | bytes 8055736 | solution.py:99
  571.0 9.6 %all-gather.3 = f32[24,8,8,16]{3,2,1,0:T(8,128)S(1)} all-gather(f32[3,8,8,16]{3,2,1,0:T(8,128)S(1)} %broadcast_select_fusion), channel_id=5, replica_groups=mesh['grp'=4,'gz'=8] {'gz'}, dimensions={0}, use_global_device_ids=true | all-gather | bytes 110592 | tf_op jit(solution)/shard_map/all_gather | solution.py:25
  588.7 44.4 %while.256 = (s32[]{:T(128)}, f32[3,9,64,128]{3,2,1,0:T(8,128)}, s32[2]{0:T(128)S(1)}, f32[3,9,64,128]{3,2,1,0:T(8,128)S(1)}, f32[8,64,128]{2,1,0:T(8,128)S(1)},...) while((s32[]{:T(128)}, f32[3,9,64,128]{3,2,1,0:T(8,128)}, ...), condition=%wide.region_37.38_spmd.clone, body=%wide.region_36.37_spmd.sunk.clone.sunk | while | flops 230057488 | bytes 52208232 | solution.py:99
  597.8 6.5 multiply_bitcast_fusion.16
  620.0 6.5 multiply_bitcast_fusion.16
  647.9 44.4 %while.257 = (s32[]{:T(128)}, f32[3,9,64,128]{3,2,1,0:T(8,128)}, s32[2]{0:T(128)S(1)}, f32[3,9,64,128]{3,2,1,0:T(8,128)S(1)}, f32[8,64,128]{2,1,0:T(8,128)S(1)},...) while((s32[]{:T(128)}, f32[3,9,64,128]{3,2,1,0:T(8,128)}, ...), condition=%wide.region_41.42_spmd.clone, body=%wide.region_40.41_spmd.sunk.clone.sunk | while | flops 230057488 | bytes 52208232 | solution.py:99
  657.0 6.5 multiply_bitcast_fusion.17
  679.2 6.5 multiply_bitcast_fusion.17
  704.1 45.2 %all-reduce.19 = (f32[]{:T(128)}, f32[]{:T(128)}) all-reduce(f32[]{:T(128)} %get-tuple-element.2477, f32[]{:T(128)} %get-tuple-element.2476), channel_id=1, replica_groups=mesh['grp'=4,'gz'=8] {'grp','gz'}, use_global_device_ids=true, to_apply=%region_39.40 | all-reduce | flops 2 | bytes 16 | tf_op jit(solution)/shard_map/psum | solution.py:151
  (1333 shorter events, 515.2 us)
Async XLA Ops:
  0.6 26.0 %copy-start.16 = (f32[24,24]{1,0:T(8,128)S(1)}, f32[24,24]{1,0:T(8,128)}, u32[]{:S(2)}) copy-start(f32[24,24]{1,0:T(8,128)} %constant.3032.clone) | copy-start | bytes 6916
  0.6 27.4 %copy-start = (f32[24,24]{1,0:T(8,128)S(1)}, f32[24,24]{1,0:T(8,128)}, u32[]{:S(2)}) copy-start(f32[24,24]{1,0:T(8,128)} %constant.3073) | copy-start | bytes 6916
  5.8 24.0 %collective-permute-start = (f32[1,64,128]{2,1,0:T(8,128)S(1)}, f32[1,64,128]{2,1,0:T(8,128)S(1)}, u32[]{:S(2)}, u32[]{:S(2)}) collective-permute-start(f32[1,64,128]{2,1,0:T(8,128)S(1)} %slice.6742), channel_id=1, source_target_pairs={{0,1},{1,2},{2,3},{3,4},{4,5},{5,6},{6,7},{7,8},{8,9},{9,10},{10,1... | collective-permute-start | bytes 98312 | tf_op jit(solution)/shard_map/ppermute | solution.py:20
  29.6 61.6 %copy-start.17 = (f32[8,64,128]{2,1,0:T(8,128)}, f32[8,64,128]{2,1,0:T(8,128)S(1)}, u32[]{:S(2)}) copy-start(f32[8,64,128]{2,1,0:T(8,128)S(1)} %get-tuple-element.2978) | copy-start | bytes 786436
  32.0 3.2 collective-permute-start.1
  36.3 50.6 %copy-start.70 = (f32[3]{0:T(128)S(1)}, f32[3]{0:T(128)}, u32[]{:S(2)}) copy-start(f32[3]{0:T(128)} %get-tuple-element.2986) | copy-start | bytes 40
  36.3 50.6 %copy-start.71 = (f32[3]{0:T(128)S(1)}, f32[3]{0:T(128)}, u32[]{:S(2)}) copy-start(f32[3]{0:T(128)} %get-tuple-element.2987) | copy-start | bytes 40
  80.5 10.7 %copy-start.5 = (f32[3,8,64,128]{3,2,1,0:T(8,128)S(1)}, f32[3,8,64,128]{3,2,1,0:T(8,128)}, u32[]{:S(2)}) copy-start(f32[3,8,64,128]{3,2,1,0:T(8,128)} %param.237) | copy-start | bytes 2359300
  81.5 8.8 %collective-permute-start.2 = (f32[3,1,64,128]{3,2,1,0:T(8,128)S(1)}, f32[3,1,64,128]{3,2,1,0:T(8,128)S(1)}, u32[]{:S(2)}, u32[]{:S(2)}) collective-permute-start(f32[3,1,64,128]{3,2,1,0:T(8,128)S(1)} %slice.5989), channel_id=1, source_target_pairs={{0,1},{1,2},{2,3},{3,4},{4,5},{5,6},{6,7},{7,8},{8,9},{9,10},{10,1... | collective-permute-start | bytes 294920 | tf_op jit(solution)/shard_map/ppermute | solution.py:20
  88.8 12.9 %copy-start.2 = (f32[3,8,8,16]{0,3,2,1:T(8,128)}, f32[3,8,8,16]{0,3,2,1:T(8,128)S(1)}, u32[]{:S(2)}) copy-start(f32[3,8,8,16]{0,3,2,1:T(8,128)S(1)} %add_divide_fusion) | copy-start | bytes 36868
  206.8 13.9 %copy-start.6 = (f32[3,8,64,128]{3,2,1,0:T(8,128)S(1)}, f32[3,8,64,128]{3,2,1,0:T(8,128)}, u32[]{:S(2)}) copy-start(f32[3,8,64,128]{3,2,1,0:T(8,128)} %param.237) | copy-start | bytes 2359300
  221.0 3.2 collective-permute-start.3
  225.3 52.6 %copy-start.18 = (f32[8,64,128]{2,1,0:T(8,128)S(1)}, f32[8,64,128]{2,1,0:T(8,128)}, u32[]{:S(2)}) copy-start(f32[8,64,128]{2,1,0:T(8,128)} %copy-done.17) | copy-start | bytes 786436
  270.4 6.6 collective-permute-start.4
  280.3 3.2 collective-permute-start.5
  328.9 57.6 %copy-start.7 = (f32[3,8,64,128]{3,2,1,0:T(8,128)S(1)}, f32[3,8,64,128]{3,2,1,0:T(8,128)}, u32[]{:S(2)}) copy-start(f32[3,8,64,128]{3,2,1,0:T(8,128)} %param.237) | copy-start | bytes 2359300
  329.9 6.7 collective-permute-start.6
  337.5 51.3 %copy-start.34 = (f32[3,8,64,128]{3,2,1,0:T(8,128)}, f32[3,8,64,128]{3,2,1,0:T(8,128)S(1)}, u32[]{:S(2)}) copy-start(f32[3,8,64,128]{3,2,1,0:T(8,128)S(1)} %add_dynamic-update-slice_fusion.21) | copy-start | bytes 2359300
  389.8 3.2 collective-permute-start.7
  439.6 12.3 %copy-start.39 = (f32[24,24,1,1]{1,0,3,2:T(8,128)}, f32[24,24,1,1]{1,0,3,2:T(8,128)S(1)}, u32[]{:S(2)}) copy-start(f32[24,24,1,1]{1,0,3,2:T(8,128)S(1)} %get-tuple-element.4566) | copy-start | bytes 6916
  440.5 6.9 collective-permute-start.8
  448.4 16.3 %copy-start.1 = (f32[24,24]{1,0:T(8,128)S(1)}, f32[24,24]{1,0:T(8,128)}, u32[]{:S(2)}) copy-start(f32[24,24]{1,0:T(8,128)} %constant.3073) | copy-start | bytes 6916
  448.4 16.2 %copy-start.3 = (f32[3,8,8,16]{0,3,2,1:T(8,128)S(1)}, f32[3,8,8,16]{0,3,2,1:T(8,128)}, u32[]{:S(2)}) copy-start(f32[3,8,8,16]{0,3,2,1:T(8,128)} %copy-done.2) | copy-start | bytes 36868
  570.0 14.1 %copy-start.8 = (f32[3,8,64,128]{3,2,1,0:T(8,128)S(1)}, f32[3,8,64,128]{3,2,1,0:T(8,128)}, u32[]{:S(2)}) copy-start(f32[3,8,64,128]{3,2,1,0:T(8,128)} %get-tuple-element.2665) | copy-start | bytes 2359300
  584.3 3.2 collective-permute-start.9
  588.7 52.5 %copy-start.19 = (f32[8,64,128]{2,1,0:T(8,128)S(1)}, f32[8,64,128]{2,1,0:T(8,128)}, u32[]{:S(2)}) copy-start(f32[8,64,128]{2,1,0:T(8,128)} %copy-done.17) | copy-start | bytes 786436
  634.0 6.2 collective-permute-start.10
  643.6 3.2 collective-permute-start.11
  647.9 54.2 %copy-start.9 = (f32[3,8,64,128]{3,2,1,0:T(8,128)S(1)}, f32[3,8,64,128]{3,2,1,0:T(8,128)}, u32[]{:S(2)}) copy-start(f32[3,8,64,128]{3,2,1,0:T(8,128)} %get-tuple-element.2665) | copy-start | bytes 2359300
  692.3 61.7 %copy-start.35 = (f32[3,8,64,128]{3,2,1,0:T(8,128)S(1)}, f32[3,8,64,128]{3,2,1,0:T(8,128)}, u32[]{:S(2)}) copy-start(f32[3,8,64,128]{3,2,1,0:T(8,128)} %copy-done.34) | copy-start | bytes 2359300
  692.3 61.7 %copy-start.36 = (f32[3,8,64,128]{3,2,1,0:T(8,128)S(1)}, f32[3,8,64,128]{3,2,1,0:T(8,128)}, u32[]{:S(2)}) copy-start(f32[3,8,64,128]{3,2,1,0:T(8,128)} %get-tuple-element.2667) | copy-start | bytes 2359300
  693.3 6.9 collective-permute-start.12
  (103 other events, 147.6 us)
